TPU v7x, 32 devices: a whole 2x2x4 slice. The times are simulated.
32 devices in a mesh: groups: 2 (over y), span: 4 (over z), head: 2 (over x), slab: 2 (over core).
Axes of the slice: x: 2, y: 2, z: 4, core: 2. Of those that a mesh axis runs over, the one named last changes fastest.
Arguments:
- queries: bfloat16 [3072, 5120], P(('groups', 'span'), 'head'), parts along dimension 0, may hold values from -6 to 6
- keys: bfloat16 [3072, 5120], P(('groups', 'span', 'slab'), 'head'), parts along dimension 0, may hold values from -4 to 4
- values: bfloat16 [3072, 5120], P(('groups', 'span', 'slab'), 'head'), parts along dimension 0, may hold values from -240 to 240
- span_mask: int32 [8, 4], P('groups'), parts along dimension 0, may hold values from 0 to 1, as said below
- head_gain: float32 [5120], P('head'), may hold values from 0.5 to 2
- head_shift: float32 [5120], P('head'), may hold values from -3 to 3
- patch_weight: bfloat16 [5120, 64], P('head'), may hold values from -0.078125 to 0.078125
- noisy_latent: float32 [24, 16, 32, 16], P(('groups', 'span'), 'head', 'slab'), parts along dimension 0, may hold values from -6 to 6
- conv_weight: bfloat16 [432, 384], replicated, may hold values from -0.3125 to 0.3125
- conv_bias: float32 [384], replicated, may hold values from -3 to 3
Outputs:
- clean_latent: float32 [24, 16, 32, 16], P(('groups', 'span'), 'head', 'slab'), parts along dimension 0
- decoded: bfloat16 [24, 16, 32, 384], P(('groups', 'span'), 'head', 'slab'), parts along dimension 0
There are 2 independent parts, one for each index of `groups`. A program takes and returns all parts, laid end to end along the dimension named above; an argument that names none is the same for every part. Nothing has to cross between parts.
Inputs may be any that keep to these rules, and one draw needn't show every extreme that they name: span_mask[i, j] is 1 where j = i and 0 where j > i.
All inputs are finite; a program needn't handle non-finite values.
Results may differ from a plain program's by a relative error of at most 0.012.
Values may be sent and summed in bfloat16 or wider, within the bound.
No kernel may reach another device: no remote copies, remote signals or barrier semaphores. Data moves between devices by JAX's collectives and lax.ppermute only.
A program may use at most 128 MiB of HBM per device.

v0:
```python
import math
import jax
import jax.numpy as jnp
from jax import lax
from jax.sharding import PartitionSpec as P

HEADS = 40
HD = 128
LAT_CH = 16
FRAMES_SPAN = 3
TROWS = 8
TCOLS = 16
neg_big = -1e30
noise_level = 0.75
norm_eps = 1e-06


def with_halo(cells, sides, width):
    for axis, dim in sides:
        count = lax.axis_size(axis)
        ends = count - 1
        head = lax.slice_in_dim(cells, 0, width, axis=dim)
        tail = lax.slice_in_dim(cells, cells.shape[dim] - width, cells.shape[dim], axis=dim)
        cells = jnp.concatenate(
            [
                lax.ppermute(tail, axis, [(i, (i + 1) % count) for i in range(ends)]),
                cells,
                lax.ppermute(head, axis, [((i + 1) % count, i) for i in range(ends)]),
            ],
            axis=dim,
        )
    return cells


def from_behind(value, axis, by):
    size = lax.axis_size(axis)
    pairs = [(i, i + by) for i in range(size) if 0 <= i + by < size]
    return lax.ppermute(value, axis, pairs)


def block_length(total_rows):
    block_size = total_rows
    while block_size > 768 and block_size % 2 == 0:
        block_size = block_size // 2
    return block_size


def fold_keys(partial_state, key_value, query_block, mask_row, rows_span):
    keys_piece, values_piece = key_value
    heads_dev = query_block.shape[1]
    piece_rows = keys_piece.shape[0]
    length = block_length(piece_rows)
    span_count = mask_row.shape[0]
    score_scale = 1.0 / math.sqrt(HD)
    span_ids = jnp.arange(span_count, dtype=jnp.int32)

    def one_block(carry_state, block_index):
        running_max, running_sum, weighted = carry_state
        offset = block_index * length
        key_block = lax.dynamic_slice_in_dim(keys_piece, offset, length, 0).reshape(
            length, heads_dev, HD
        )
        value_block = lax.dynamic_slice_in_dim(values_piece, offset, length, 0).reshape(
            length, heads_dev, HD
        )
        key_span = (offset + jnp.arange(length, dtype=jnp.int32)) // rows_span
        allowed = (
            jnp.sum(jnp.where(key_span[:, None] == span_ids[None, :], mask_row[None, :], 0), axis=1)
            > 0
        )
        scores = (
            jnp.einsum("qhd,khd->hqk", query_block, key_block, preferred_element_type=jnp.float32)
            * score_scale
        )
        scores = jnp.where(allowed[None, None, :], scores, neg_big)
        new_max = jnp.maximum(running_max, jnp.max(scores, axis=2))
        weights = jnp.where(allowed[None, None, :], jnp.exp(scores - new_max[:, :, None]), 0.0)
        factor = jnp.exp(running_max - new_max)
        running_sum = running_sum * factor + jnp.sum(weights, axis=2)
        weighted = weighted * factor.T[:, :, None] + jnp.einsum(
            "hqk,khd->qhd",
            weights.astype(jnp.bfloat16),
            value_block,
            preferred_element_type=jnp.float32,
        )
        return ((new_max, running_sum, weighted), None)

    result, unused = lax.scan(
        one_block, partial_state, jnp.arange(piece_rows // length, dtype=jnp.int32)
    )
    return result


def per_device(
    queries,
    keys,
    values,
    span_mask,
    head_gain,
    head_shift,
    patch_weight,
    noisy_latent,
    conv_weight,
    conv_bias,
):
    heads_dev = queries.shape[1] // HD
    slab_count = lax.axis_size("slab")
    col_dev = TCOLS // slab_count
    slab_place = lax.axis_index("slab")
    span_place = lax.axis_index("span")
    mask_row = lax.dynamic_slice_in_dim(span_mask, span_place, 1, 0)[0]
    token_grid = queries.reshape(FRAMES_SPAN, TROWS, TCOLS, queries.shape[-1])
    picked = lax.dynamic_slice_in_dim(token_grid, slab_place * col_dev, col_dev, 2)
    own_queries = picked.reshape(FRAMES_SPAN * TROWS * col_dev, queries.shape[-1]).reshape(
        -1, heads_dev, HD
    )
    query_rows = own_queries.shape[0]
    rows_span = keys.shape[0] * slab_count
    running_max, running_sum, weighted = fold_keys(
        (
            jnp.full((heads_dev, query_rows), neg_big, jnp.float32),
            jnp.zeros((heads_dev, query_rows), jnp.float32),
            jnp.zeros((query_rows, heads_dev, HD), jnp.float32),
        ),
        (
            lax.all_gather(keys, ("span", "slab"), axis=0, tiled=True),
            lax.all_gather(values, ("span", "slab"), axis=0, tiled=True),
        ),
        own_queries,
        mask_row,
        rows_span,
    )
    attended = (
        (weighted / running_sum.T[:, :, None])
        .astype(jnp.bfloat16)
        .reshape(query_rows, heads_dev * HD)
    )
    feature_width = HEADS * HD
    values32 = attended.astype(jnp.float32)
    row_total = jnp.sum(values32, axis=1)
    row_squares = jnp.sum(values32 * values32, axis=1)
    row_total, row_squares = lax.psum((row_total, row_squares), "head")
    row_mean = row_total / feature_width
    spread = row_squares / feature_width - row_mean * row_mean
    normed = (
        (values32 - row_mean[:, None]) * lax.rsqrt(spread + norm_eps)[:, None] * head_gain[None, :]
        + head_shift[None, :]
    ).astype(jnp.bfloat16)
    normed_grid = normed.reshape(FRAMES_SPAN, TROWS, col_dev, normed.shape[-1])
    own_rows = TROWS // lax.axis_size("head")
    picked = normed_grid
    product = jnp.dot(
        picked.reshape(-1, picked.shape[-1]), patch_weight, preferred_element_type=jnp.float32
    )
    velocity = lax.psum_scatter(
        product.reshape(
            FRAMES_SPAN, own_rows * lax.axis_size("head"), col_dev * patch_weight.shape[1]
        )
        .transpose(1, 0, 2)
        .reshape(own_rows * lax.axis_size("head"), -1)
        .astype(jnp.bfloat16),
        "head",
        scatter_dimension=0,
        tiled=True,
    ).astype(jnp.float32)
    rows_dev = velocity.shape[0]
    patch_cells = (
        velocity.reshape(rows_dev, FRAMES_SPAN, col_dev, 2, 2, LAT_CH)
        .transpose(1, 0, 3, 2, 4, 5)
        .reshape(FRAMES_SPAN, 2 * rows_dev, 2 * col_dev, LAT_CH)
    )
    clean_latent = noisy_latent - noise_level * patch_cells
    latent_input = clean_latent.astype(jnp.bfloat16)
    framed = with_halo(latent_input, (("head", 1), ("slab", 2)), 1)
    earlier = from_behind(framed[FRAMES_SPAN - 2 :], "span", 1)
    stacked = jnp.concatenate([earlier, framed], axis=0)
    height = clean_latent.shape[1]
    breadth = clean_latent.shape[2]
    columns = jnp.concatenate(
        [
            stacked[
                frame_tap : frame_tap + FRAMES_SPAN,
                row_tap : row_tap + height,
                col_tap : col_tap + breadth,
                :,
            ]
            for frame_tap in range(3)
            for row_tap in range(3)
            for col_tap in range(3)
        ],
        axis=-1,
    )
    decoded = (
        jnp.dot(
            columns.reshape(FRAMES_SPAN * height * breadth, 27 * LAT_CH),
            conv_weight,
            preferred_element_type=jnp.float32,
        )
        + conv_bias[None, :]
    )
    decoded = decoded.astype(jnp.bfloat16).reshape(
        FRAMES_SPAN, height, breadth, conv_weight.shape[1]
    )
    return (clean_latent, decoded)


def solution(mesh):
    placed = (
        P(("groups", "span"), "head"),
        P(("groups", "span", "slab"), "head"),
        P(("groups", "span", "slab"), "head"),
        P("groups", None),
        P("head"),
        P("head"),
        P("head", None),
        P(("groups", "span"), "head", "slab", None),
        P(),
        P(),
    )
    return jax.shard_map(
        per_device,
        mesh=mesh,
        in_specs=placed,
        out_specs=(
            P(("groups", "span"), "head", "slab", None),
            P(("groups", "span"), "head", "slab", None),
        ),
        check_vma=False,
    )
```

profile of v0, /device:TPU:0, one launch (start us, length us, event | category | flops | bytes accessed | tf_op | source)
XLA Modules:
  0.0 286.9 jit_solution(14048511079382129699)
XLA Ops:
  9.8 1.7 reshape_reshape.3
  14.6 75.5 %all-gather.3.cloned.1.call-done = bf16[1536,2560]{1,0:T(8,128)(2,1)} async-done(((bf16[192,2560]{1,0:T(8,128)(2,1)}), bf16[1536,2560]{1,0:T(8,128)(2,1)}) %all-gather.3.cloned.1.call-update) | async-done | bytes 7864336 | tf_op jit(solution)/shard_map/all_gather | solution.py:126
  90.1 78.0 %all-gather.5.cloned.1.call-done = bf16[1536,2560]{1,0:T(8,128)(2,1)} async-done(((bf16[192,2560]{1,0:T(8,128)(2,1)}), bf16[1536,2560]{1,0:T(8,128)(2,1)}) %all-gather.5.cloned.1.call-update) | async-done | bytes 7864336 | tf_op jit(solution)/shard_map/all_gather | solution.py:127
  168.1 70.0 %while.17 = (s32[]{:T(128)}, f32[20,192]{1,0:T(8,128)S(1)}, f32[20,192]{1,0:T(8,128)S(1)}, f32[192,20,128]{2,0,1:T(8,128)}, s32[2]{0:T(128)S(1)}, /*index=5*/s32...) while((s32[]{:T(128)}, f32[20,192]{1,0:T(8,128)S(1)}, ...), condition=%wide.region_4.5_spmd.clone, body=%wide.region_0.4_spmd.clone.sunk | while | flops 1549801728 | bytes 95616248 | solution.py:88
  169.5 7.0 %constant_dynamic-slice_fusion.5 = (bf16[768,2560]{1,0:T(8,128)(2,1)}, bf16[768,2560]{1,0:T(8,128)(2,1)}) fusion(bf16[1536,2560]{1,0:T(8,128)(2,1)} %get-tuple-element.368, s32[]{:T(128)S(6)} %select_n.93, bf16[1536,2560]{1,0:T(8,128)(2,1)} %get-tuple-element.366), kind=kLoop, calls=%fused_computation.26.clone.1 | loop fusion | bytes 15728644 | tf_op jit(solution)/shard_map/while/body/eval_jaxpr/dynamic_slice | solution.py:63
  176.4 6.3 %copy.52 = bf16[768,2560]{0,1:T(8,128)(2,1)} copy(bf16[768,2560]{1,0:T(8,128)(2,1)} %get-tuple-element.328) | data formatting | bytes 7864320 | tf_op jit(solution)/shard_map/while/body/eval_jaxpr/dynamic_slice | solution.py:60
  182.7 6.3 %copy.53 = bf16[768,2560]{0,1:T(8,128)(2,1)} copy(bf16[768,2560]{1,0:T(8,128)(2,1)} %get-tuple-element.332) | data formatting | bytes 7864320 | tf_op jit(solution)/shard_map/while/body/eval_jaxpr/dynamic_slice | solution.py:63
  189.0 4.8 %bitcast_reduce_fusion.2 = (f32[20,192]{1,0:T(8,128)S(1)}, f32[20,768,192]{1,2,0:T(8,128)S(1)}) fusion(pred[768]{0:T(1024)(128)(4,1)S(1)} %broadcast_compare_fusion.2, bf16[192,20,128]{2,0,1:T(8,128)(2,1)} %get-tuple-element.367, bf16[768,20,128]{0,2,1:T(8,128)(2,1)} %bitcast.80), kind=kOutput, calls=%fused_computation.2.clone.1 | convolution fusion | flops 763818240 | bytes 16727808 | tf_op jit(solution)/shard_map/while/body/eval_jaxpr/qhd,khd->hqk/dot_general | solution.py:72
  193.8 4.8 %bitcast_add_fusion.2 = f32[192,20,128]{2,0,1:T(8,128)} fusion(f32[192,20,128]{2,0,1:T(8,128)} %get-tuple-element.350, bf16[768,20,128]{0,2,1:T(8,128)(2,1)S(1)} %bitcast.81, f32[20,768,192]{1,2,0:T(8,128)S(1)} %get-tuple-element.331, f32[20,192]{1,0:T(8,128)S(1)} %get-tuple-element.361, pred[768]{0:T(1024)(128)(4,1)S(1)} %broadcast_compare_fusion.2, ...), kind=kOutput, calls=%fused_computation.11.clone.1 | convolution fusion | flops 771194880 | bytes 19692288 | tf_op jit(solution)/shard_map/while/body/eval_jaxpr/hqk,khd->qhd/dot_general | solution.py:80
  198.6 3.6 %fusion.51 = f32[20,192]{1,0:T(8,128)S(1)} fusion(f32[20,768,192]{1,2,0:T(8,128)S(1)} %get-tuple-element.331, f32[20,192]{1,0:T(8,128)S(1)} %get-tuple-element.361, pred[768]{0:T(1024)(128)(4,1)S(1)} %broadcast_compare_fusion.2), kind=kLoop, calls=%fused_computation.7.clone.1 | loop fusion | flops 14741760 | bytes 11827968 | tf_op jit(solution)/shard_map/while/body/eval_jaxpr/reduce_sum | solution.py:79
  203.7 7.0 %constant_dynamic-slice_fusion.5 = (bf16[768,2560]{1,0:T(8,128)(2,1)}, bf16[768,2560]{1,0:T(8,128)(2,1)}) fusion(bf16[1536,2560]{1,0:T(8,128)(2,1)} %get-tuple-element.368, s32[]{:T(128)S(6)} %select_n.93, bf16[1536,2560]{1,0:T(8,128)(2,1)} %get-tuple-element.366), kind=kLoop, calls=%fused_computation.26.clone.1 | loop fusion | bytes 15728644 | tf_op jit(solution)/shard_map/while/body/eval_jaxpr/dynamic_slice | solution.py:63
  210.6 6.3 %copy.52 = bf16[768,2560]{0,1:T(8,128)(2,1)} copy(bf16[768,2560]{1,0:T(8,128)(2,1)} %get-tuple-element.328) | data formatting | bytes 7864320 | tf_op jit(solution)/shard_map/while/body/eval_jaxpr/dynamic_slice | solution.py:60
  216.9 6.3 %copy.53 = bf16[768,2560]{0,1:T(8,128)(2,1)} copy(bf16[768,2560]{1,0:T(8,128)(2,1)} %get-tuple-element.332) | data formatting | bytes 7864320 | tf_op jit(solution)/shard_map/while/body/eval_jaxpr/dynamic_slice | solution.py:63
  223.2 4.8 %bitcast_reduce_fusion.2 = (f32[20,192]{1,0:T(8,128)S(1)}, f32[20,768,192]{1,2,0:T(8,128)S(1)}) fusion(pred[768]{0:T(1024)(128)(4,1)S(1)} %broadcast_compare_fusion.2, bf16[192,20,128]{2,0,1:T(8,128)(2,1)} %get-tuple-element.367, bf16[768,20,128]{0,2,1:T(8,128)(2,1)} %bitcast.80), kind=kOutput, calls=%fused_computation.2.clone.1 | convolution fusion | flops 763818240 | bytes 16727808 | tf_op jit(solution)/shard_map/while/body/eval_jaxpr/qhd,khd->hqk/dot_general | solution.py:72
  228.0 6.4 %bitcast_add_fusion.2 = f32[192,20,128]{2,0,1:T(8,128)} fusion(f32[192,20,128]{2,0,1:T(8,128)} %get-tuple-element.350, bf16[768,20,128]{0,2,1:T(8,128)(2,1)S(1)} %bitcast.81, f32[20,768,192]{1,2,0:T(8,128)S(1)} %get-tuple-element.331, f32[20,192]{1,0:T(8,128)S(1)} %get-tuple-element.361, pred[768]{0:T(1024)(128)(4,1)S(1)} %broadcast_compare_fusion.2, ...), kind=kOutput, calls=%fused_computation.11.clone.1 | convolution fusion | flops 771194880 | bytes 19692288 | tf_op jit(solution)/shard_map/while/body/eval_jaxpr/hqk,khd->qhd/dot_general | solution.py:80
  234.4 3.6 %fusion.51 = f32[20,192]{1,0:T(8,128)S(1)} fusion(f32[20,768,192]{1,2,0:T(8,128)S(1)} %get-tuple-element.331, f32[20,192]{1,0:T(8,128)S(1)} %get-tuple-element.361, pred[768]{0:T(1024)(128)(4,1)S(1)} %broadcast_compare_fusion.2), kind=kLoop, calls=%fused_computation.7.clone.1 | loop fusion | flops 14741760 | bytes 11827968 | tf_op jit(solution)/shard_map/while/body/eval_jaxpr/reduce_sum | solution.py:79
  238.1 2.2 convert_reduce_fusion
  240.4 4.9 %all-reduce.1 = (f32[192]{0:T(256)S(1)}, f32[192]{0:T(256)S(1)}) all-reduce(f32[192]{0:T(256)S(1)} %get-tuple-element.200, f32[192]{0:T(256)S(1)} %get-tuple-element.199), channel_id=1, replica_groups=mesh['groups'=2,'span'=4,'head'=2,'slab'=2] {'head'}, use_global_device_ids=true, to_apply=%region_8.9 | all-reduce | flops 384 | bytes 3072 | tf_op jit(solution)/shard_map/psum | solution.py:142
  247.1 8.3 %all-reduce = bf16[8,1536]{1,0:T(8,128)(2,1)S(1)} all-reduce(bf16[8,1536]{1,0:T(8,128)(2,1)S(1)} %bitcast.86), channel_id=2, replica_groups=mesh['groups'=2,'span'=4,'head'=2,'slab'=2] {'head'}, use_global_device_ids=true, to_apply=%region_9.10.clone | all-reduce | flops 12288 | bytes 49152
  256.6 2.4 collective-permute-start
  260.4 4.2 %collective-permute-done.1 = bf16[3,1,16,16]{3,2,1,0:T(8,128)(2,1)S(1)} collective-permute-done((bf16[3,1,16,16]{3,2,1,0:T(8,128)(2,1)S(1)}, bf16[3,1,16,16]{3,2,1,0:T(8,128)(2,1)S(1)}, u32[]{:S(2)}, u32[]{:S(2)}) %collective-permute-start.1) | collective-permute-done | bytes 1568 | tf_op jit(solution)/shard_map/ppermute | solution.py:28
  271.3 2.2 collective-permute-done.4
  274.6 3.2 %concatenate.35 = bf16[3,8,16,432]{3,2,1,0:T(8,128)(2,1)} concatenate(bf16[3,8,16,16]{3,2,1,0:T(8,128)(2,1)} %get-tuple-element.247, bf16[3,8,16,16]{3,2,1,0:T(8,128)(2,1)} %get-tuple-element.246, bf16[3,8,16,16]{3,2,1,0:T(8,128)(2,1)} %get-tuple-element.245, bf16[3,8,16,16]{3,2,1,0:T(8,128)(2,1)S(1)} %get-tuple-element.244, bf16[3,8,16,16]{3,2,1,0:T(8,128)(2,1)S(1)} %get-tuple-element.243, ...), dimensions={3} | concatenate | bytes 663552 | tf_op jit(solution)/shard_map/concatenate | solution.py:179
  277.8 2.2 fusion.23
  (65 shorter events, 18.6 us)
Async XLA Ops:
  7.2 1.6 copy-start
  7.2 5.5 %copy-start.6 = (u32[32]{0:T(128)S(1)}, u32[32]{0:T(128)}, u32[]{:S(2)}) copy-start(u32[32]{0:T(128)} %constant.95) | copy-start | bytes 388
  7.2 82.9 %all-gather.3.cloned.1.call-start = ((), (), s32[]{:S(2)}) async-start(), calls=%async_computation | async-start | bytes 8847360 | tf_op jit(solution)/shard_map/all_gather | solution.py:126
  7.9 160.2 %all-gather.5.cloned.1.call-start = ((), (), s32[]{:S(2)}) async-start(), calls=%async_computation.1 | async-start | bytes 8847360 | tf_op jit(solution)/shard_map/all_gather | solution.py:127
  168.1 77.2 %copy-start.3 = (f32[2560]{0:T(1024)S(1)}, f32[2560]{0:T(1024)}, u32[]{:S(2)}) copy-start(f32[2560]{0:T(1024)} %param.17) | copy-start | bytes 30724
  168.1 77.2 %copy-start.4 = (f32[2560]{0:T(1024)S(1)}, f32[2560]{0:T(1024)}, u32[]{:S(2)}) copy-start(f32[2560]{0:T(1024)} %param.16) | copy-start | bytes 30724
  189.0 4.8 %copy-start.1 = (bf16[768,2560]{0,1:T(8,128)(2,1)S(1)}, bf16[768,2560]{0,1:T(8,128)(2,1)}, u32[]{:S(2)}) copy-start(bf16[768,2560]{0,1:T(8,128)(2,1)} %copy.53) | copy-start | bytes 11796484 | tf_op jit(solution)/shard_map/while
  223.2 4.8 %copy-start.1 = (bf16[768,2560]{0,1:T(8,128)(2,1)S(1)}, bf16[768,2560]{0,1:T(8,128)(2,1)}, u32[]{:S(2)}) copy-start(bf16[768,2560]{0,1:T(8,128)(2,1)} %copy.53) | copy-start | bytes 11796484 | tf_op jit(solution)/shard_map/while
  238.1 17.7 %copy-start.2 = (f32[3,8,16,16]{3,2,1,0:T(8,128)S(1)}, f32[3,8,16,16]{3,2,1,0:T(8,128)}, u32[]{:S(2)}) copy-start(f32[3,8,16,16]{3,2,1,0:T(8,128)} %param.19) | copy-start | bytes 73732
  256.6 3.8 %collective-permute-start = (bf16[3,1,16,16]{3,2,1,0:T(8,128)(2,1)S(1)}, bf16[3,1,16,16]{3,2,1,0:T(8,128)(2,1)S(1)}, u32[]{:S(2)}, u32[]{:S(2)}) collective-permute-start(bf16[3,1,16,16]{3,2,1,0:T(8,128)(2,1)S(1)} %get-tuple-element.260), channel_id=1, source_target_pairs={{0,2},{1,3},{4,6},{5,7},{8,10},{9,11},{12,14},{13,15},{16,18},{17,... | collective-permute-start | bytes 4616 | tf_op jit(solution)/shard_map/ppermute | solution.py:26
  259.0 5.6 %collective-permute-start.1 = (bf16[3,1,16,16]{3,2,1,0:T(8,128)(2,1)S(1)}, bf16[3,1,16,16]{3,2,1,0:T(8,128)(2,1)S(1)}, u32[]{:S(2)}, u32[]{:S(2)}) collective-permute-start(bf16[3,1,16,16]{3,2,1,0:T(8,128)(2,1)S(1)} %get-tuple-element.261), channel_id=1, source_target_pairs={{2,0},{3,1},{6,4},{7,5},{10,8},{11,9},{14,12},{15,13},{18,16},{19,... | collective-permute-start | bytes 4616 | tf_op jit(solution)/shard_map/ppermute | solution.py:28
  264.6 3.3 %collective-permute-start.2 = (bf16[3,10,1,16]{3,2,1,0:T(2,128)(2,1)S(1)}, bf16[3,10,1,16]{3,2,1,0:T(2,128)(2,1)S(1)}, u32[]{:S(2)}, u32[]{:S(2)}) collective-permute-start(bf16[3,10,1,16]{3,2,1,0:T(2,128)(2,1)S(1)} %get-tuple-element.256), channel_id=1, source_target_pairs={{0,1},{2,3},{4,5},{6,7},{8,9},{10,11},{12,13},{14,15},{16,17},{18,... | collective-permute-start | bytes 2888 | tf_op jit(solution)/shard_map/ppermute | solution.py:26
  265.9 3.1 %collective-permute-start.3 = (bf16[3,10,1,16]{3,2,1,0:T(2,128)(2,1)S(1)}, bf16[3,10,1,16]{3,2,1,0:T(2,128)(2,1)S(1)}, u32[]{:S(2)}, u32[]{:S(2)}) collective-permute-start(bf16[3,10,1,16]{3,2,1,0:T(2,128)(2,1)S(1)} %get-tuple-element.257), channel_id=1, source_target_pairs={{1,0},{3,2},{5,4},{7,6},{9,8},{11,10},{13,12},{15,14},{17,16},{19,... | collective-permute-start | bytes 2888 | tf_op jit(solution)/shard_map/ppermute | solution.py:28
  269.1 4.5 %collective-permute-start.4 = (bf16[2,10,18,16]{3,2,1,0:T(8,128)(2,1)S(1)}, bf16[2,10,18,16]{3,2,1,0:T(8,128)(2,1)S(1)}, u32[]{:S(2)}, u32[]{:S(2)}) collective-permute-start(bf16[2,10,18,16]{3,2,1,0:T(8,128)(2,1)S(1)} %pad_maximum_fusion.1), channel_id=1, source_target_pairs={{0,4},{4,8},{8,12},{1,5},{5,9},{9,13},{2,6},{6,10},{10,14},{3,7},{... | collective-permute-start | bytes 34568 | tf_op jit(solution)/shard_map/ppermute | solution.py:38
  270.5 7.4 %copy-start.5 = (f32[384]{0:T(512)S(1)}, f32[384]{0:T(512)}, u32[]{:S(2)}) copy-start(f32[384]{0:T(512)} %param.21) | copy-start | bytes 4612
Sparse Core Ops, SparseCore 0:
  9.7 80.4 all-gather.2
  91.8 76.2 all-gather.4
where the time goes:
time: 288 us; the launch traced here: 287 us
  waiting for transfers between devices  162 us (56%)
  local copies, waits for them, and re-layouts  51.2 us (18%)
  matrix products  24.5 us (9%)
  between operations  14.9 us (5%)
  blocking collectives  13.3 us (5%)
  other arithmetic  11.5 us (4%)
  starting transfers between devices  7.64 us (3%)
    all_gather x1, waiting for transfers between devices, per_device(): lax.all_gather(values, ('span', 'slab'), axis=0, tiled=True)  78 us
    all_gather x1, waiting for transfers between devices, per_device(): lax.all_gather(keys, ('span', 'slab'), axis=0, tiled=True)  75.5 us
    dynamic_slice x4, local copies, waits for them, and re-layouts, one_block(): lax.dynamic_slice_in_dim(values_piece, offset, length, 0)  26.6 us
    dynamic_slice x2, local copies, waits for them, and re-layouts, one_block(): lax.dynamic_slice_in_dim(keys_piece, offset, length, 0)  12.6 us
    dot_general x2, matrix products, one_block(): jnp.einsum('hqk,khd->qhd', weights.astype(jnp.bfloat16), value_block, pre...  11.2 us
    dot_general x2, matrix products, one_block(): jnp.einsum('qhd,khd->hqk', query_block, key_block, preferred_element_type...  9.52 us
    unnamed x1, blocking collectives  8.32 us
    reduce_sum x2, other arithmetic, one_block(): running_sum = running_sum * factor + jnp.sum(weights, axis=2)  7.25 us
  transfers between devices with their start and end apart: 7, of which 6 were waited for; matrix products, arithmetic and copies ran while one was open for 2% of the time, Pallas kernels for 0%

commit v1 on v0

--- a/solution.py
+++ b/solution.py
@@ -13,6 +13,27 @@
 neg_big = -1e30
 noise_level = 0.75
 norm_eps = 1e-06
+
+
+def ring_gather(x, axis, dim):
+    length, index, span = (lax.axis_size(axis), lax.axis_index(axis), x.shape[dim])
+    right = [(i, (i + 1) % length) for i in range(length)]
+    backward = [(i, (i - 1) % length) for i in range(length)]
+    filled = jnp.zeros((*x.shape[:dim], length * span, *x.shape[dim + 1 :]), x.dtype)
+    filled = lax.dynamic_update_slice_in_dim(filled, x, index * span, axis=dim)
+    from_left = from_right = x
+    halfway = length // 2
+    for lap in range(1, halfway + 1):
+        from_left = lax.ppermute(from_left, axis, right)
+        filled = lax.dynamic_update_slice_in_dim(
+            filled, from_left, (index - lap) % length * span, axis=dim
+        )
+        if lap < length - halfway:
+            from_right = lax.ppermute(from_right, axis, backward)
+            filled = lax.dynamic_update_slice_in_dim(
+                filled, from_right, (index + lap) % length * span, axis=dim
+            )
+    return filled
 
 
 def with_halo(cells, sides, width):
@@ -123,7 +144,7 @@
             jnp.zeros((query_rows, heads_dev, HD), jnp.float32),
         ),
         (
-            lax.all_gather(keys, ("span", "slab"), axis=0, tiled=True),
+            ring_gather(keys, ("span", "slab"), 0),
             lax.all_gather(values, ("span", "slab"), axis=0, tiled=True),
         ),
         own_queries,

time: 288 us -> 373 us (1.30)
  local copies, waits for them, and re-layouts: 51.2 us -> 160 us
  waiting for transfers between devices: 162 us -> 107 us
  starting transfers between devices: 7.64 us -> 41.8 us
  matrix products: 24.5 us -> 18.7 us
    dynamic_update_slice x0 -> x8, local copies, waits for them, and re-layouts: none -> 105 us  [the longest x4 51.8 us: ring_gather(): lax.dynamic_update_slice_in_dim(filled, from_left, (index - lap) % length...]
    ppermute x0 -> x7, waiting for transfers between devices: none -> 99.1 us  [the longest x4 80.1 us: ring_gather(): from_left = lax.ppermute(from_left, axis, right)]
    all_gather x1, waiting for transfers between devices: 78 us -> 0.01 us  [per_device(): lax.all_gather(values, ('span', 'slab'), axis=0, tiled=True)]
    all_gather x1 -> x0, waiting for transfers between devices: 75.5 us -> none  [per_device(): lax.all_gather(keys, ('span', 'slab'), axis=0, tiled=True)]
    ppermute x0 -> x7, starting transfers between devices: none -> 21.8 us  [the longest x3 11.6 us: ring_gather(): from_right = lax.ppermute(from_right, axis, backward)]
    ppermute x1, starting transfers between devices: 1.3 us -> 14.2 us  [from_behind(): return lax.ppermute(value, axis, pairs)]
    ppermute x0 -> x7, local copies, waits for them, and re-layouts: none -> 9.77 us  [the longest x4 6.13 us: ring_gather(): from_left = lax.ppermute(from_left, axis, right)]
    dynamic_slice x2, local copies, waits for them, and re-layouts: 12.6 us -> 4.73 us  [one_block(): lax.dynamic_slice_in_dim(keys_piece, offset, length, 0)]
  transfers between devices with their start and end apart: 7 -> 13, of which waited for: 6 -> 9; matrix products, arithmetic and copies ran while one was open for 2% -> 35% of each run, Pallas kernels for 0% -> 0%
where the time goes in v1:
time: 373 us; the launch traced here: 369 us
  local copies, waits for them, and re-layouts  160 us (43%)
  waiting for transfers between devices  107 us (29%)
  starting transfers between devices  41.8 us (11%)
  matrix products  18.7 us (5%)
  between operations  15 us (4%)
  blocking collectives  13.9 us (4%)
  other arithmetic  11.5 us (3%)
    ppermute x4, waiting for transfers between devices, ring_gather(): from_left = lax.ppermute(from_left, axis, right)  80.1 us
    dynamic_update_slice x4, local copies, waits for them, and re-layouts, ring_gather(): lax.dynamic_update_slice_in_dim(filled, from_left, (index - lap) % length...  51.8 us
    dynamic_update_slice x3, local copies, waits for them, and re-layouts, ring_gather(): lax.dynamic_update_slice_in_dim(filled, from_right, (index + lap) % lengt...  40.5 us
    dynamic_slice x4, local copies, waits for them, and re-layouts, one_block(): lax.dynamic_slice_in_dim(values_piece, offset, length, 0)  21 us
    ppermute x3, waiting for transfers between devices, ring_gather(): from_right = lax.ppermute(from_right, axis, backward)  18.9 us
    ppermute x1, starting transfers between devices, from_behind(): return lax.ppermute(value, axis, pairs)  14.2 us
    dynamic_update_slice x1, local copies, waits for them, and re-layouts, ring_gather(): filled = lax.dynamic_update_slice_in_dim(filled, x, index * span, axis=dim)  12.6 us
    ppermute x3, starting transfers between devices, ring_gather(): from_right = lax.ppermute(from_right, axis, backward)  11.6 us
  transfers between devices with their start and end apart: 13, of which 9 were waited for; matrix products, arithmetic and copies ran while one was open for 35% of the time, Pallas kernels for 0%

profile of v1, /device:TPU:0, one launch (start us, length us, event | category | flops | bytes accessed | tf_op | source)
XLA Modules:
  0.0 369.2 jit_solution(13091725520436589946)
XLA Ops:
  12.5 26.8 %collective-permute-done = bf16[192,2560]{1,0:T(8,128)(2,1)S(1)} collective-permute-done((bf16[192,2560]{1,0:T(8,128)(2,1)}, bf16[192,2560]{1,0:T(8,128)(2,1)S(1)}, u32[]{:S(2)}, u32[]{:S(2)}) %collective-permute-start) | collective-permute-done | bytes 983072 | tf_op jit(solution)/shard_map/ppermute | solution.py:27
  40.2 7.6 %collective-permute-done.1 = bf16[192,2560]{1,0:T(8,128)(2,1)S(1)} collective-permute-done((bf16[192,2560]{1,0:T(8,128)(2,1)}, bf16[192,2560]{1,0:T(8,128)(2,1)S(1)}, u32[]{:S(2)}, u32[]{:S(2)}) %collective-permute-start.1) | collective-permute-done | bytes 983072 | tf_op jit(solution)/shard_map/ppermute | solution.py:32
  52.4 29.5 %collective-permute-done.2 = bf16[192,2560]{1,0:T(8,128)(2,1)S(1)} collective-permute-done((bf16[192,2560]{1,0:T(8,128)(2,1)S(1)}, bf16[192,2560]{1,0:T(8,128)(2,1)S(1)}, u32[]{:S(2)}, u32[]{:S(2)}) %collective-permute-start.2) | collective-permute-done | bytes 983072 | tf_op jit(solution)/shard_map/ppermute | solution.py:27
  83.2 11.3 %collective-permute-done.3 = bf16[192,2560]{1,0:T(8,128)(2,1)} collective-permute-done((bf16[192,2560]{1,0:T(8,128)(2,1)S(1)}, bf16[192,2560]{1,0:T(8,128)(2,1)}, u32[]{:S(2)}, u32[]{:S(2)}) %collective-permute-start.3) | collective-permute-done | bytes 983072 | tf_op jit(solution)/shard_map/ppermute | solution.py:32
  98.4 23.8 %collective-permute-done.4 = bf16[192,2560]{1,0:T(8,128)(2,1)} collective-permute-done((bf16[192,2560]{1,0:T(8,128)(2,1)S(1)}, bf16[192,2560]{1,0:T(8,128)(2,1)}, u32[]{:S(2)}, u32[]{:S(2)}) %collective-permute-start.4) | collective-permute-done | bytes 983072 | tf_op jit(solution)/shard_map/ppermute | solution.py:27
  122.2 7.6 %collective-permute-start.6 = (bf16[192,2560]{1,0:T(8,128)(2,1)}, bf16[192,2560]{1,0:T(8,128)(2,1)}, u32[]{:S(2)}, u32[]{:S(2)}) collective-permute-start(bf16[192,2560]{1,0:T(8,128)(2,1)} %collective-permute-done.4), channel_id=1, source_target_pairs={{0,1},{1,4},{4,5},{5,8},{8,9},{9,12},{12,13},{13,0},{2,3},{3,6},{6... | collective-permute-start | bytes 2949128 | tf_op jit(solution)/shard_map/ppermute | solution.py:27
  141.3 12.6 %dynamic_update_slice.24 = bf16[1536,2560]{0,1:T(8,128)(2,1)} dynamic-update-slice(bf16[1536,2560]{0,1:T(8,128)(2,1)} %broadcast_in_dim.80, bf16[192,2560]{0,1:T(8,128)(2,1)S(1)} %copy.48, s32[]{:T(128)S(6)} %select_n.104, s32[]{:T(128)} %constant.123.clone.1) | dynamic-update-slice | bytes 1966084 | tf_op jit(solution)/shard_map/dynamic_update_slice | solution.py:23
  156.2 13.2 %dynamic_update_slice.25 = bf16[1536,2560]{0,1:T(8,128)(2,1)} dynamic-update-slice(bf16[1536,2560]{0,1:T(8,128)(2,1)} %dynamic_update_slice.24, bf16[192,2560]{0,1:T(8,128)(2,1)S(1)} %copy.49, s32[]{:T(128)S(6)} %select_n.106, s32[]{:T(128)} %constant.123.clone.1) | dynamic-update-slice | bytes 1966084 | tf_op jit(solution)/shard_map/dynamic_update_slice | solution.py:28
  170.0 14.0 %dynamic_update_slice.26 = bf16[1536,2560]{0,1:T(8,128)(2,1)} dynamic-update-slice(bf16[1536,2560]{0,1:T(8,128)(2,1)} %dynamic_update_slice.25, bf16[192,2560]{0,1:T(8,128)(2,1)S(1)} %copy.50, s32[]{:T(128)S(6)} %select_n.108, s32[]{:T(128)} %constant.123.clone.1) | dynamic-update-slice | bytes 1966084 | tf_op jit(solution)/shard_map/dynamic_update_slice | solution.py:33
  185.5 12.2 %dynamic_update_slice.27 = bf16[1536,2560]{0,1:T(8,128)(2,1)} dynamic-update-slice(bf16[1536,2560]{0,1:T(8,128)(2,1)} %dynamic_update_slice.26, bf16[192,2560]{0,1:T(8,128)(2,1)S(1)} %copy.51, s32[]{:T(128)S(6)} %select_n.110, s32[]{:T(128)} %constant.123.clone.1) | dynamic-update-slice | bytes 1966084 | tf_op jit(solution)/shard_map/dynamic_update_slice | solution.py:28
  199.2 12.5 %dynamic_update_slice.28 = bf16[1536,2560]{0,1:T(8,128)(2,1)} dynamic-update-slice(bf16[1536,2560]{0,1:T(8,128)(2,1)} %dynamic_update_slice.27, bf16[192,2560]{0,1:T(8,128)(2,1)S(1)} %copy.52, s32[]{:T(128)S(6)} %select_n.112, s32[]{:T(128)} %constant.123.clone.1) | dynamic-update-slice | bytes 1966084 | tf_op jit(solution)/shard_map/dynamic_update_slice | solution.py:33
  213.3 14.0 %dynamic_update_slice.29 = bf16[1536,2560]{0,1:T(8,128)(2,1)} dynamic-update-slice(bf16[1536,2560]{0,1:T(8,128)(2,1)} %dynamic_update_slice.28, bf16[192,2560]{0,1:T(8,128)(2,1)S(1)} %copy.53, s32[]{:T(128)S(6)} %select_n.114, s32[]{:T(128)} %constant.123.clone.1) | dynamic-update-slice | bytes 1966084 | tf_op jit(solution)/shard_map/dynamic_update_slice | solution.py:28
  228.8 14.0 %dynamic_update_slice.30 = bf16[1536,2560]{0,1:T(8,128)(2,1)} dynamic-update-slice(bf16[1536,2560]{0,1:T(8,128)(2,1)} %dynamic_update_slice.29, bf16[192,2560]{0,1:T(8,128)(2,1)S(1)} %copy.54, s32[]{:T(128)S(6)} %select_n.116, s32[]{:T(128)} %constant.123.clone.1) | dynamic-update-slice | bytes 1966084 | tf_op jit(solution)/shard_map/dynamic_update_slice | solution.py:33
  244.3 12.5 %dynamic_update_slice.31 = bf16[1536,2560]{0,1:T(8,128)(2,1)} dynamic-update-slice(bf16[1536,2560]{0,1:T(8,128)(2,1)} %dynamic_update_slice.30, bf16[192,2560]{0,1:T(8,128)(2,1)S(1)} %copy.55, s32[]{:T(128)S(6)} %select_n.118, s32[]{:T(128)} %constant.123.clone.1) | dynamic-update-slice | bytes 1966084 | tf_op jit(solution)/shard_map/dynamic_update_slice | solution.py:28
  256.8 51.8 %while.17 = (s32[]{:T(128)}, f32[20,192]{1,0:T(8,128)S(1)}, f32[20,192]{1,0:T(8,128)S(1)}, f32[192,20,128]{2,0,1:T(8,128)}, s32[2]{0:T(128)S(1)}, /*index=5*/s32...) while((s32[]{:T(128)}, f32[20,192]{1,0:T(8,128)S(1)}, ...), condition=%wide.region_4.5_spmd.clone, body=%wide.region_0.4_spmd.clone.sunk | while | flops 1549801728 | bytes 87751936 | solution.py:109
  258.2 4.2 %constant_dynamic-slice_fusion.7 = bf16[768,2560]{1,0:T(8,128)(2,1)} fusion(bf16[1536,2560]{1,0:T(8,128)(2,1)} %get-tuple-element.362, s32[]{:T(128)S(6)} %select_n.163), kind=kLoop, calls=%fused_computation.26.clone.1 | loop fusion | bytes 7864324 | tf_op jit(solution)/shard_map/while/body/eval_jaxpr/dynamic_slice | solution.py:84
  262.4 6.3 %copy.68 = bf16[768,2560]{0,1:T(8,128)(2,1)} copy(bf16[768,2560]{1,0:T(8,128)(2,1)} %constant_dynamic-slice_fusion.7) | data formatting | bytes 7864320 | tf_op jit(solution)/shard_map/while/body/eval_jaxpr/dynamic_slice | solution.py:84
  273.4 4.8 %bitcast_add_fusion.2 = f32[192,20,128]{2,0,1:T(8,128)} fusion(f32[192,20,128]{2,0,1:T(8,128)} %get-tuple-element.344, bf16[768,20,128]{0,2,1:T(8,128)(2,1)S(1)} %bitcast.81, f32[20,768,192]{1,2,0:T(8,128)S(1)} %get-tuple-element.326, f32[20,192]{1,0:T(8,128)S(1)} %get-tuple-element.355, pred[768]{0:T(1024)(128)(4,1)S(1)} %broadcast_compare_fusion.2, ...), kind=kOutput, calls=%fused_computation.11.clone.1 | convolution fusion | flops 771194880 | bytes 19692288 | tf_op jit(solution)/shard_map/while/body/eval_jaxpr/hqk,khd->qhd/dot_general | solution.py:101
  283.2 4.2 %constant_dynamic-slice_fusion.7 = bf16[768,2560]{1,0:T(8,128)(2,1)} fusion(bf16[1536,2560]{1,0:T(8,128)(2,1)} %get-tuple-element.362, s32[]{:T(128)S(6)} %select_n.163), kind=kLoop, calls=%fused_computation.26.clone.1 | loop fusion | bytes 7864324 | tf_op jit(solution)/shard_map/while/body/eval_jaxpr/dynamic_slice | solution.py:84
  287.5 6.3 %copy.68 = bf16[768,2560]{0,1:T(8,128)(2,1)} copy(bf16[768,2560]{1,0:T(8,128)(2,1)} %constant_dynamic-slice_fusion.7) | data formatting | bytes 7864320 | tf_op jit(solution)/shard_map/while/body/eval_jaxpr/dynamic_slice | solution.py:84
  298.5 6.5 %bitcast_add_fusion.2 = f32[192,20,128]{2,0,1:T(8,128)} fusion(f32[192,20,128]{2,0,1:T(8,128)} %get-tuple-element.344, bf16[768,20,128]{0,2,1:T(8,128)(2,1)S(1)} %bitcast.81, f32[20,768,192]{1,2,0:T(8,128)S(1)} %get-tuple-element.326, f32[20,192]{1,0:T(8,128)S(1)} %get-tuple-element.355, pred[768]{0:T(1024)(128)(4,1)S(1)} %broadcast_compare_fusion.2, ...), kind=kOutput, calls=%fused_computation.11.clone.1 | convolution fusion | flops 771194880 | bytes 19692288 | tf_op jit(solution)/shard_map/while/body/eval_jaxpr/hqk,khd->qhd/dot_general | solution.py:101
  310.8 5.1 %all-reduce.1 = (f32[192]{0:T(256)S(1)}, f32[192]{0:T(256)S(1)}) all-reduce(f32[192]{0:T(256)S(1)} %get-tuple-element.200, f32[192]{0:T(256)S(1)} %get-tuple-element.199), channel_id=1, replica_groups=mesh['groups'=2,'span'=4,'head'=2,'slab'=2] {'head'}, use_global_device_ids=true, to_apply=%region_8.9 | all-reduce | flops 384 | bytes 3072 | tf_op jit(solution)/shard_map/psum | solution.py:163
  316.8 8.8 %all-reduce = bf16[8,1536]{1,0:T(8,128)(2,1)S(1)} all-reduce(bf16[8,1536]{1,0:T(8,128)(2,1)S(1)} %bitcast.86), channel_id=2, replica_groups=mesh['groups'=2,'span'=4,'head'=2,'slab'=2] {'head'}, use_global_device_ids=true, to_apply=%region_9.10.clone | all-reduce | flops 12288 | bytes 49152
  338.8 14.2 %collective-permute-start.11 = (bf16[2,10,18,16]{3,2,1,0:T(8,128)(2,1)S(1)}, bf16[2,10,18,16]{3,2,1,0:T(8,128)(2,1)S(1)}, u32[]{:S(2)}, u32[]{:S(2)}) collective-permute-start(bf16[2,10,18,16]{3,2,1,0:T(8,128)(2,1)S(1)} %pad_maximum_fusion.1), channel_id=1, source_target_pairs={{0,4},{4,8},{8,12},{1,5},{5,9},{9,13},{2,6},{6,10},{10,14},{3,7},{... | collective-permute-start | bytes 34568 | tf_op jit(solution)/shard_map/ppermute | solution.py:59
  (105 shorter events, 80.7 us)
Async XLA Ops:
  7.2 124.2 %copy-start = (bf16[384,2560]{1,0:T(8,128)(2,1)S(1)}, bf16[384,2560]{1,0:T(8,128)(2,1)}, u32[]{:S(2)}) copy-start(bf16[384,2560]{1,0:T(8,128)(2,1)} %param.12) | copy-start | bytes 5898244
  7.2 249.6 %all-gather.2.cloned.1.call-start = ((), (), s32[]{:S(2)}) async-start(), calls=%async_computation | async-start | bytes 8847360 | tf_op jit(solution)/shard_map/all_gather | solution.py:148
  7.9 31.5 %collective-permute-start = (bf16[192,2560]{1,0:T(8,128)(2,1)}, bf16[192,2560]{1,0:T(8,128)(2,1)S(1)}, u32[]{:S(2)}, u32[]{:S(2)}) collective-permute-start(bf16[192,2560]{1,0:T(8,128)(2,1)} %param.13), channel_id=1, source_target_pairs={{0,1},{1,4},{4,5},{5,8},{8,9},{9,12},{12,13},{13,0},{2,3},{3,6},{6... | collective-permute-start | bytes 2949128 | tf_op jit(solution)/shard_map/ppermute | solution.py:27
  8.4 39.3 %collective-permute-start.1 = (bf16[192,2560]{1,0:T(8,128)(2,1)}, bf16[192,2560]{1,0:T(8,128)(2,1)S(1)}, u32[]{:S(2)}, u32[]{:S(2)}) collective-permute-start(bf16[192,2560]{1,0:T(8,128)(2,1)} %param.13), channel_id=1, source_target_pairs={{0,13},{1,0},{4,1},{5,4},{8,5},{9,8},{12,9},{13,12},{2,15},{3,2},{... | collective-permute-start | bytes 2949128 | tf_op jit(solution)/shard_map/ppermute | solution.py:32
  39.4 82.8 %copy-start.6 = (bf16[192,2560]{1,0:T(8,128)(2,1)}, bf16[192,2560]{1,0:T(8,128)(2,1)S(1)}, u32[]{:S(2)}) copy-start(bf16[192,2560]{1,0:T(8,128)(2,1)S(1)} %collective-permute-done) | copy-start | bytes 2949124
  39.4 42.5 %collective-permute-start.2 = (bf16[192,2560]{1,0:T(8,128)(2,1)S(1)}, bf16[192,2560]{1,0:T(8,128)(2,1)S(1)}, u32[]{:S(2)}, u32[]{:S(2)}) collective-permute-start(bf16[192,2560]{1,0:T(8,128)(2,1)S(1)} %collective-permute-done), channel_id=1, source_target_pairs={{0,1},{1,4},{4,5},{5,8},{8,9},{9,12},{12,13},{13,0},{2,3},{3,6},{6... | collective-permute-start | bytes 2949128 | tf_op jit(solution)/shard_map/ppermute | solution.py:27
  48.7 45.8 %collective-permute-start.3 = (bf16[192,2560]{1,0:T(8,128)(2,1)S(1)}, bf16[192,2560]{1,0:T(8,128)(2,1)}, u32[]{:S(2)}, u32[]{:S(2)}) collective-permute-start(bf16[192,2560]{1,0:T(8,128)(2,1)S(1)} %collective-permute-done.1), channel_id=1, source_target_pairs={{0,13},{1,0},{4,1},{5,4},{8,5},{9,8},{12,9},{13,12},{2,15},{3,2},{... | collective-permute-start | bytes 2949128 | tf_op jit(solution)/shard_map/ppermute | solution.py:32
  81.8 12.7 %copy-start.5 = (bf16[192,2560]{1,0:T(8,128)(2,1)}, bf16[192,2560]{1,0:T(8,128)(2,1)S(1)}, u32[]{:S(2)}) copy-start(bf16[192,2560]{1,0:T(8,128)(2,1)S(1)} %collective-permute-done.2) | copy-start | bytes 2949124
  81.8 40.4 %collective-permute-start.4 = (bf16[192,2560]{1,0:T(8,128)(2,1)S(1)}, bf16[192,2560]{1,0:T(8,128)(2,1)}, u32[]{:S(2)}, u32[]{:S(2)}) collective-permute-start(bf16[192,2560]{1,0:T(8,128)(2,1)S(1)} %collective-permute-done.2), channel_id=1, source_target_pairs={{0,1},{1,4},{4,5},{5,8},{8,9},{9,12},{12,13},{13,0},{2,3},{3,6},{6... | collective-permute-start | bytes 2949128 | tf_op jit(solution)/shard_map/ppermute | solution.py:27
  94.5 132.7 %collective-permute-start.5 = (bf16[192,2560]{1,0:T(8,128)(2,1)}, bf16[192,2560]{1,0:T(8,128)(2,1)}, u32[]{:S(2)}, u32[]{:S(2)}) collective-permute-start(bf16[192,2560]{1,0:T(8,128)(2,1)} %collective-permute-done.3), channel_id=1, source_target_pairs={{0,13},{1,0},{4,1},{5,4},{8,5},{9,8},{12,9},{13,12},{2,15},{3,2},{... | collective-permute-start | bytes 2949128 | tf_op jit(solution)/shard_map/ppermute | solution.py:32
  122.2 120.6 %collective-permute-start.6 = (bf16[192,2560]{1,0:T(8,128)(2,1)}, bf16[192,2560]{1,0:T(8,128)(2,1)}, u32[]{:S(2)}, u32[]{:S(2)}) collective-permute-start(bf16[192,2560]{1,0:T(8,128)(2,1)} %collective-permute-done.4), channel_id=1, source_target_pairs={{0,1},{1,4},{4,5},{5,8},{8,9},{9,12},{12,13},{13,0},{2,3},{3,6},{6... | collective-permute-start | bytes 2949128 | tf_op jit(solution)/shard_map/ppermute | solution.py:27
  129.8 6.6 %copy-start.12 = (u32[32]{0:T(128)S(1)}, u32[32]{0:T(128)}, u32[]{:S(2)}) copy-start(u32[32]{0:T(128)} %constant.149) | copy-start | bytes 388
  141.3 28.0 %copy-start.4 = (bf16[192,2560]{1,0:T(8,128)(2,1)S(1)}, bf16[192,2560]{1,0:T(8,128)(2,1)}, u32[]{:S(2)}) copy-start(bf16[192,2560]{1,0:T(8,128)(2,1)} %copy-done.3) | copy-start | bytes 2949124
  256.8 59.2 %copy-start.8 = (bf16[2560,64]{0,1:T(8,128)(2,1)S(1)}, bf16[2560,64]{0,1:T(8,128)(2,1)}, u32[]{:S(2)}) copy-start(bf16[2560,64]{0,1:T(8,128)(2,1)} %param.18) | copy-start | bytes 983044
  256.8 59.2 %copy-start.9 = (f32[2560]{0:T(1024)S(1)}, f32[2560]{0:T(1024)}, u32[]{:S(2)}) copy-start(f32[2560]{0:T(1024)} %param.17) | copy-start | bytes 30724
  256.8 59.2 %copy-start.10 = (f32[2560]{0:T(1024)S(1)}, f32[2560]{0:T(1024)}, u32[]{:S(2)}) copy-start(f32[2560]{0:T(1024)} %param.16) | copy-start | bytes 30724
  308.6 17.4 %copy-start.7 = (f32[3,8,16,16]{3,2,1,0:T(8,128)S(1)}, f32[3,8,16,16]{3,2,1,0:T(8,128)}, u32[]{:S(2)}) copy-start(f32[3,8,16,16]{3,2,1,0:T(8,128)} %param.19) | copy-start | bytes 73732
  326.7 3.3 collective-permute-start.7
  328.7 5.6 %collective-permute-start.8 = (bf16[3,1,16,16]{3,2,1,0:T(8,128)(2,1)S(1)}, bf16[3,1,16,16]{3,2,1,0:T(8,128)(2,1)S(1)}, u32[]{:S(2)}, u32[]{:S(2)}) collective-permute-start(bf16[3,1,16,16]{3,2,1,0:T(8,128)(2,1)S(1)} %get-tuple-element.259), channel_id=1, source_target_pairs={{2,0},{3,1},{6,4},{7,5},{10,8},{11,9},{14,12},{15,13},{18,16},{19,... | collective-permute-start | bytes 4616 | tf_op jit(solution)/shard_map/ppermute | solution.py:49
  334.3 3.3 collective-permute-start.9
  335.6 3.1 collective-permute-start.10
  338.8 17.1 %collective-permute-start.11 = (bf16[2,10,18,16]{3,2,1,0:T(8,128)(2,1)S(1)}, bf16[2,10,18,16]{3,2,1,0:T(8,128)(2,1)S(1)}, u32[]{:S(2)}, u32[]{:S(2)}) collective-permute-start(bf16[2,10,18,16]{3,2,1,0:T(8,128)(2,1)S(1)} %pad_maximum_fusion.1), channel_id=1, source_target_pairs={{0,4},{4,8},{8,12},{1,5},{5,9},{9,13},{2,6},{6,10},{10,14},{3,7},{... | collective-permute-start | bytes 34568 | tf_op jit(solution)/shard_map/ppermute | solution.py:59
  353.0 7.1 %copy-start.11 = (f32[384]{0:T(512)S(1)}, f32[384]{0:T(512)}, u32[]{:S(2)}) copy-start(f32[384]{0:T(512)} %param.21) | copy-start | bytes 4612
  355.8 6.5 %copy-start.1 = (bf16[384,2560]{1,0:T(8,128)(2,1)S(1)}, bf16[384,2560]{1,0:T(8,128)(2,1)}, u32[]{:S(2)}) copy-start(bf16[384,2560]{1,0:T(8,128)(2,1)} %param.12) | copy-start | bytes 5898244
  (3 other events, 5.6 us)
Sparse Core Ops, SparseCore 0:
  9.7 130.5 all-gather.1
